TPU v7x, 1024 devices: a whole 4x4x32 slice. The times are simulated.
1024 devices in a mesh: grp: 16 (over y, x), mdl: 64 (over z, core).
Axes of the slice: x: 4, y: 4, z: 32, core: 2. Of those that a mesh axis runs over, the one named last changes fastest.
Arguments:
- enc_out: bfloat16 [5120, 8192], P('grp'), may hold values from -6 to 6
- w_key: bfloat16 [8192, 8192], P(None, 'mdl'), may hold values from -0.0625 to 0.0625
- w_value: bfloat16 [8192, 8192], P(None, 'mdl'), may hold values from -0.0625 to 0.0625
- queries: bfloat16 [24576, 8192], P('grp', 'mdl'), may hold values from -600 to 600
- src_len: int32 [16, 19], replicated, may hold values from 1 to 48, as said below
- tgt_len: int32 [304], replicated, may hold values from 1 to 48, as said below
- destination: int32 [304, 1], replicated, may hold values from 0 to 15
Outputs:
- context: bfloat16 [24576, 8192], P('grp', 'mdl')
- variance: float32 [], replicated
Inputs may be any that keep to these rules, and one draw needn't show every extreme that they name: `src_len`: the sentences of one encoder shard fill its 320 rows, one of them has 48 rows, and the sentences of one shard with one destination have at most 96 source rows, reached by some group for every shard. `tgt_len`: the sentences of one shard with one destination have as many target rows in all as source rows.
All inputs are finite; a program needn't handle non-finite values.
Results may differ from a plain program's by a relative error of at most 0.024.
Values may be sent and summed in bfloat16 or wider, within the bound.
A program may use at most 32 MiB of HBM per device.

v0:
```python
import jax
import jax.numpy as jnp
from jax import lax
from jax.sharding import PartitionSpec as P

HEAD_DIM = 128
CAP = 96
SENTS = 19


def layout(lengths, groups_of, wanted):
    going = (groups_of == wanted[:, None]).astype(jnp.int32)
    sent = lengths * going
    pair_start = jnp.cumsum(sent, axis=1) - sent
    rows = jnp.arange(CAP, dtype=jnp.int32)[None, :, None]
    above = (rows >= pair_start[:, None, :]).astype(jnp.int32)
    below = (rows < (pair_start + lengths)[:, None, :]).astype(jnp.int32)
    return (going[:, None, :] * above * below, pair_start)


def describe(member):
    numbers = jnp.arange(member.shape[2], dtype=jnp.int32)
    return (jnp.sum(member, axis=2), jnp.sum(member * numbers[None, None, :], axis=2))


def per_device(enc_out, w_key, w_value, queries, src_len, tgt_len, destination):
    group = lax.axis_index("grp")
    shards = lax.axis_size("grp")
    width = w_key.shape[1]
    local_heads = width // HEAD_DIM
    key_states = jnp.dot(enc_out, w_key, preferred_element_type=jnp.float32).astype(jnp.bfloat16)
    value_states = jnp.dot(enc_out, w_value, preferred_element_type=jnp.float32).astype(
        jnp.bfloat16
    )
    packed = jnp.concatenate([key_states, value_states], axis=1)
    groups_of = destination.reshape(shards, SENTS)
    starts = jnp.cumsum(src_len, axis=1) - src_len
    targets = tgt_len.reshape(shards, SENTS)
    shard_ids = jnp.arange(shards, dtype=jnp.int32)
    rows = jnp.arange(CAP, dtype=jnp.int32)
    wanted = jnp.zeros((shards,), jnp.int32) + group
    member_src, pair_src = layout(src_len, groups_of, wanted)
    k_live, k_seg = describe(member_src)
    member_tgt, pair_tgt = layout(targets, groups_of, wanted)
    q_live, q_seg = describe(member_tgt)
    own_groups = lax.dynamic_index_in_dim(groups_of, group, 0, keepdims=False)
    own_starts = lax.dynamic_index_in_dim(starts, group, 0, keepdims=False)
    own_lengths = lax.dynamic_index_in_dim(src_len, group, 0, keepdims=False)
    tiled_lengths = jnp.broadcast_to(own_lengths[None, :], (shards, SENTS))
    tiled_groups = jnp.broadcast_to(own_groups[None, :], (shards, SENTS))
    send_member, send_start = layout(tiled_lengths, tiled_groups, shard_ids)
    send_live, send_seg = describe(send_member)
    send_offset = (
        jnp.sum(send_member * (own_starts[None, :] - send_start)[:, None, :], axis=2)
        + rows[None, :]
    )
    send_index = jnp.clip(send_offset, 0, packed.shape[0] - 1)
    outgoing = jnp.take(packed, send_index.reshape(-1), axis=0).reshape(shards, CAP, 2 * width)
    outgoing = jnp.where(send_live[:, :, None] > 0, outgoing, jnp.zeros_like(outgoing))
    incoming = lax.all_to_all(outgoing, "grp", split_axis=0, concat_axis=0, tiled=True)
    key_block = incoming[..., :width].reshape(shards, CAP, local_heads, HEAD_DIM)
    value_block = incoming[..., width:].reshape(shards, CAP, local_heads, HEAD_DIM)
    query_block = queries.reshape(shards, CAP, local_heads, HEAD_DIM)
    scores = jnp.einsum(
        "eqhd,ekhd->ehqk", query_block, key_block, preferred_element_type=jnp.float32
    ) * HEAD_DIM ** (-0.5)
    allowed = (
        (q_live[:, :, None] > 0)
        & (k_live[:, None, :] > 0)
        & (q_seg[:, :, None] == k_seg[:, None, :])
    )
    allowed = allowed[:, None]
    scores = jnp.where(allowed, scores, -1e30)
    top = jnp.max(scores, axis=-1, keepdims=True)
    powers = jnp.where(allowed, jnp.exp(scores - top), 0.0)
    dead = (1 - q_live).astype(jnp.float32)[:, None, :, None]
    total = jnp.sum(powers, axis=-1, keepdims=True) + dead
    weights = (powers / total).astype(jnp.bfloat16)
    attended = jnp.einsum(
        "ehqk,ekhd->eqhd", weights, value_block, preferred_element_type=jnp.float32
    )
    attended = attended * q_live.astype(jnp.float32)[:, :, None, None]
    context = attended.reshape(queries.shape[0], width).astype(jnp.bfloat16)
    squares = lax.psum(jnp.sum(attended * attended), ("grp", "mdl"))
    full_width = jnp.float32(width * lax.axis_size("mdl"))
    variance = squares / (full_width * jnp.sum(tgt_len).astype(jnp.float32))
    return (context, variance)


def solution(mesh):
    return jax.shard_map(
        per_device,
        mesh=mesh,
        in_specs=(P("grp", None), P(None, "mdl"), P(None, "mdl"), P("grp", "mdl"), P(), P(), P()),
        out_specs=(P("grp", "mdl"), P()),
        check_vma=False,
    )
```

profile of v0, /device:TPU:1, one launch (start us, length us, event | category | flops | bytes accessed | tf_op | source)
XLA Modules:
  0.0 212.7 jit_solution(18024101770382217259)
XLA Ops:
  0.6 0.0 copy-start
  0.6 0.8 reduce.5
  1.5 0.1 reshape.298
  1.6 0.9 reduce_window_sum.23
  2.5 0.7 fusion.21
  3.2 0.2 reduce_window_sum.22
  3.3 0.1 copy.11
  3.4 0.1 copy.10
  3.5 0.1 copy.13
  3.6 0.1 copy.12
  3.7 0.2 fusion.12
  4.0 0.1 min.12
  4.1 0.0 copy-done
  4.1 0.0 copy-start.1
  4.1 0.0 copy-start.2
  4.1 4.2 %convolution_convert_fusion = bf16[320,128]{1,0:T(8,128)(2,1)S(1)} fusion(bf16[320,8192]{1,0:T(8,128)(2,1)} %param.7, bf16[8192,128]{1,0:T(8,128)(2,1)S(1)} %copy-done), kind=kOutput, calls=%fused_computation.10 | convolution fusion | flops 671129600 | bytes 7421952 | tf_op jit(solution)/shard_map/dot_general | solution.py:32
  8.3 0.0 copy-done.1
  8.3 0.5 copy-done.2
  8.8 1.5 convolution_convert_fusion.1
  10.4 4.8 %gather_fusion = bf16[1536,256]{1,0:T(8,128)(2,1)S(1)} fusion(bf16[320,256]{1,0:T(8,128)(2,1)S(1)} %pad_maximum_fusion, s32[2048]{0:T(1024)S(1)} %pad_clamp_fusion), kind=kCustom, calls=%fused_computation | custom fusion | bytes 1579008 | tf_op jit(solution)/shard_map/jit(_take)/gather | solution.py:58
  15.1 0.0 copy-start.4
  15.2 0.0 copy-start.3
  15.2 0.0 copy-start.5
  15.2 1.3 select_select_fusion
  16.5 7.6 %all-to-all-start = ((bf16[16,96,256]{2,1,0:T(8,128)(2,1)}), bf16[16,96,256]{2,1,0:T(8,128)(2,1)S(1)}, u32[]{:S(2)}, u32[]{:S(2)}) async-start(bf16[16,96,256]{2,1,0:T(8,128)(2,1)} %select_select_fusion), calls=%async_computation | async-start | bytes 1572864 | tf_op jit(solution)/shard_map/all_to_all | solution.py:60
  24.1 0.0 copy-done.4
  24.1 0.1 reshape.299
  24.2 0.6 reduce_sum.89
  24.8 0.2 reduce_window_sum.27
  25.0 0.0 copy-done.3
  25.0 0.2 reduce_window_sum.32
  25.2 0.1 copy.17
  25.3 0.1 copy.18
  25.4 0.1 copy.14
  25.5 0.1 copy.15
  25.5 0.1 copy.16
  25.6 0.3 fusion.10
  26.6 7.9 %all-to-all-done = bf16[16,96,256]{2,1,0:T(8,128)(2,1)S(1)} async-done(((bf16[16,96,256]{2,1,0:T(8,128)(2,1)}), bf16[16,96,256]{2,1,0:T(8,128)(2,1)S(1)}, u32[]{:S(2)}, u32[]{:S(2)}) %all-to-all-start) | async-done | bytes 786464 | tf_op jit(solution)/shard_map/all_to_all | solution.py:60
  34.5 0.0 copy-done.5
  34.5 1.4 fusion.5
  35.9 1.9 fusion.26
  37.8 3.8 %multiply_reduce_fusion = (f32[]{:T(128)}, bf16[16,1,128,96]{2,3,0,1:T(8,128)(2,1)}) fusion(f32[16,96]{1,0:T(8,128)S(1)} %convert_element_type.63, f32[16,96]{1,0:T(8,128)S(1)} %convert_add_fusion, f32[16,96,96]{1,2,0:T(8,128)} %fusion.5, s32[16,96]{1,0:T(8,128)S(1)} %get-tuple-element.3, s32[16,96]{1,0:T(8,128)S(1)} %get-tuple-element.9, ...), kind=kOutput, calls=%fused_computation.12 | convolution fusion | flops 39568992 | bytes 2396164 | tf_op jit(solution)/shard_map/ehqk,ekhd->eqhd/dot_general | solution.py:79
  41.6 169.4 %psum.7 = f32[]{:T(128)} all-reduce(f32[]{:T(128)} %get-tuple-element.18), channel_id=1, replica_groups=mesh['grp'=16,'mdl'=64] {'grp','mdl'}, use_global_device_ids=true, to_apply=%region_13.14 | all-reduce | flops 1 | bytes 8 | tf_op jit(solution)/shard_map/psum | solution.py:84
  (18 shorter events, 0.2 us)
Async XLA Ops:
  0.6 3.5 %copy-start = (bf16[8192,128]{1,0:T(8,128)(2,1)S(1)}, bf16[8192,128]{1,0:T(8,128)(2,1)}, u32[]{:S(2)}) copy-start(bf16[8192,128]{1,0:T(8,128)(2,1)} %param.9) | copy-start | bytes 6291460
  4.1 4.2 %copy-start.1 = (bf16[320,8192]{1,0:T(8,128)(2,1)S(1)}, bf16[320,8192]{1,0:T(8,128)(2,1)}, u32[]{:S(2)}) copy-start(bf16[320,8192]{1,0:T(8,128)(2,1)} %param.7) | copy-start | bytes 15728644
  4.1 4.7 %copy-start.2 = (bf16[8192,128]{1,0:T(8,128)(2,1)S(1)}, bf16[8192,128]{1,0:T(8,128)(2,1)}, u32[]{:S(2)}) copy-start(bf16[8192,128]{1,0:T(8,128)(2,1)} %param.8) | copy-start | bytes 6291460
  15.1 9.0 %copy-start.4 = (s32[304]{0:T(512)S(1)}, s32[304]{0:T(512)}, u32[]{:S(2)}) copy-start(s32[304]{0:T(512)} %param.12) | copy-start | bytes 3652
  15.2 9.9 %copy-start.3 = (s32[16,19]{1,0:T(8,128)S(1)}, s32[16,19]{1,0:T(8,128)}, u32[]{:S(2)}) copy-start(s32[16,19]{1,0:T(8,128)} %param.11) | copy-start | bytes 3652
  15.2 19.4 %copy-start.5 = (bf16[1536,128]{1,0:T(8,128)(2,1)S(1)}, bf16[1536,128]{1,0:T(8,128)(2,1)}, u32[]{:S(2)}) copy-start(bf16[1536,128]{1,0:T(8,128)(2,1)} %param.10) | copy-start | bytes 1179652
  16.5 18.0 %all-to-all-start = ((bf16[16,96,256]{2,1,0:T(8,128)(2,1)}), bf16[16,96,256]{2,1,0:T(8,128)(2,1)S(1)}, u32[]{:S(2)}, u32[]{:S(2)}) async-start(bf16[16,96,256]{2,1,0:T(8,128)(2,1)} %select_select_fusion), calls=%async_computation | async-start | bytes 1572864 | tf_op jit(solution)/shard_map/all_to_all | solution.py:60
where the time goes:
time: 213 us
  blocking collectives  169 us (79%)
  matrix products  10.8 us (5%)
  waiting for transfers between devices  7.94 us (4%)
  starting transfers between devices  7.58 us (4%)
  other arithmetic  7.39 us (3%)
  local copies, waits for them, and re-layouts  6.32 us (3%)
  between operations  3.29 us (2%)
    psum x1, blocking collectives, per_device(): squares = lax.psum(jnp.sum(attended * attended), ('grp', 'mdl'))  169 us
    all_to_all x1, waiting for transfers between devices, per_device(): lax.all_to_all(outgoing, 'grp', split_axis=0, concat_axis=0, tiled=True)  7.94 us
    all_to_all x1, starting transfers between devices, per_device(): lax.all_to_all(outgoing, 'grp', split_axis=0, concat_axis=0, tiled=True)  7.58 us
    gather x1, local copies, waits for them, and re-layouts, per_device(): jnp.take(packed, send_index.reshape(-1), axis=0)  4.76 us
  transfers between devices with their start and end apart: 1, of which 1 were waited for; matrix products, arithmetic and copies ran while one was open for 1% of the time, Pallas kernels for 0%

commit v1 on v0

v1 whole, which is shorter than its diff:
```python
import functools
import math

import jax
import jax.numpy as jnp
from jax import lax
from jax.experimental import pallas as pl
from jax.experimental.pallas import tpu as pltpu
from jax.sharding import PartitionSpec as P

HEAD_DIM = 128
CAP = 96
SENTS = 19
CHUNKS = 8
BATCH = 4
MESH = pl.DeviceIdType.MESH
SCALE = math.log2(math.e) * HEAD_DIM**-0.5


def kernel(
    ng, nm, ni,
    enc, wk, wv, q, src, tgt, dst,
    ctx, var,
    enc_v, w_v, q_v, c_v, seg_v, r1, r2, r3, src_s, tgt_s, dst_s,
    load_sem, small_sem, qs_sem, qr_sem, cs_sem, cr_sem, own_sem,
    s1_sem, t1_sem, s2_sem, t2_sem, s3_sem, t3_sem,
):
    me = lax.axis_index("grp")
    mm = lax.axis_index("mdl")
    rows, depth = enc.shape
    kc = depth // CHUNKS
    no = nm // ni

    small = [
        pltpu.make_async_copy(a, b, small_sem.at[i])
        for i, (a, b) in enumerate(((src, src_s), (tgt, tgt_s), (dst, dst_s)))
    ]
    for copy in small:
        copy.start()

    def loads(c):
        part = pl.ds(c * kc, kc)
        return (
            pltpu.make_async_copy(enc.at[:, part], enc_v.at[c], load_sem.at[0, c]),
            pltpu.make_async_copy(wk.at[part], w_v.at[part, pl.ds(0, HEAD_DIM)], load_sem.at[1, c]),
            pltpu.make_async_copy(
                wv.at[part], w_v.at[part, pl.ds(HEAD_DIM, HEAD_DIM)], load_sem.at[2, c]
            ),
        )

    own_rows = pl.ds(pl.multiple_of(me * CAP, 32), CAP)
    own_q = pltpu.make_async_copy(q.at[own_rows], q_v.at[0], own_sem.at[0])
    own_q.start()
    for c in range(CHUNKS):
        for copy in loads(c):
            copy.start()

    def grp_peer(d):
        return {"grp": lax.rem(me + d, ng)}

    inner, outer = lax.rem(mm, ni), mm // ni

    def in_peer(d):
        return {"mdl": outer * ni + lax.rem(inner + d, ni)}

    def out_peer(d):
        return {"mdl": lax.rem(outer + d, no) * ni + inner}

    barrier = pltpu.get_barrier_semaphore()
    for d in range(1, ng):
        pl.semaphore_signal(barrier, inc=1, device_id=grp_peer(d), device_id_type=MESH)
    for d in range(1, ni):
        pl.semaphore_signal(barrier, inc=1, device_id=in_peer(d), device_id_type=MESH)
    for d in range(1, no):
        pl.semaphore_signal(barrier, inc=1, device_id=out_peer(d), device_id_type=MESH)
    pl.semaphore_wait(barrier, (ng - 1) + (ni - 1) + (no - 1))

    def query_copy(d):
        peer = lax.rem(me + d, ng)
        return pltpu.make_async_remote_copy(
            src_ref=q.at[pl.ds(pl.multiple_of(peer * CAP, 32), CAP)],
            dst_ref=q_v.at[d],
            send_sem=qs_sem.at[d],
            recv_sem=qr_sem.at[d],
            device_id={"grp": peer},
            device_id_type=MESH,
        )

    for d in range(1, ng):
        query_copy(d).start()

    for copy in small:
        copy.wait()
    slot = lax.broadcasted_iota(jnp.int32, seg_v.shape[::-1], 0)
    lane = lax.broadcasted_iota(jnp.int32, seg_v.shape[::-1], 1)
    group_of = lax.rem(me + ng - slot % ng, ng)
    key_row = lax.broadcasted_iota(jnp.int32, (1, rows), 1)
    seg_q = jnp.full(slot.shape, -1.0, jnp.float32)
    seg_k = jnp.zeros((1, rows), jnp.float32)
    filled = jnp.zeros(slot.shape, jnp.int32)
    start = jnp.int32(0)
    for i in range(SENTS):
        count = tgt_s[me * SENTS + i]
        going = group_of == dst_s[0, me * SENTS + i]
        after = jnp.where(going, filled + count, filled)
        seg_q = jnp.where((lane >= filled) & (lane < after), float(i), seg_q)
        filled = after
        seg_k = jnp.where(key_row >= start, float(i), seg_k)
        start = start + src_s[me, i]
    side = seg_v.shape[0]
    eye = (
        lax.broadcasted_iota(jnp.int32, (side, side), 0)
        == lax.broadcasted_iota(jnp.int32, (side, side), 1)
    ).astype(jnp.float32).astype(jnp.bfloat16)
    seg_v[...] = lax.dot_general(
        eye, seg_q.astype(jnp.bfloat16), (((1,), (1,)), ((), ())),
        preferred_element_type=jnp.float32,
    )
    live_rows = lax.fori_loop(
        0, tgt.shape[0], lambda i, t: t + tgt_s[i], jnp.int32(0), unroll=8
    )

    total = jnp.zeros((rows, 2 * HEAD_DIM), jnp.float32)
    for c in range(CHUNKS):
        for copy in loads(c):
            copy.wait()
        total = total + jnp.dot(
            enc_v[c], w_v[pl.ds(c * kc, kc), :], preferred_element_type=jnp.float32
        )
    keys = total[:, :HEAD_DIM].astype(jnp.bfloat16)
    values = jnp.concatenate(
        [total[:, HEAD_DIM:].astype(jnp.bfloat16), jnp.ones((rows, HEAD_DIM), jnp.bfloat16)], axis=1
    )

    def context_copy(d):
        return pltpu.make_async_remote_copy(
            src_ref=c_v.at[d],
            dst_ref=ctx.at[own_rows],
            send_sem=cs_sem.at[d],
            recv_sem=cr_sem.at[d],
            device_id={"grp": lax.rem(me + ng - d, ng)},
            device_id_type=MESH,
        )

    squares = jnp.zeros((8, HEAD_DIM), jnp.float32)
    own_c = pltpu.make_async_copy(c_v.at[0], ctx.at[own_rows], own_sem.at[1])
    for first in range(0, ng, BATCH):
        slots = range(first, first + BATCH)
        for d in slots:
            if d == 0:
                own_q.wait()
            else:
                query_copy(d).wait_recv()
        block = q_v[first : first + BATCH].reshape(BATCH * CAP, HEAD_DIM)
        seg = jnp.concatenate([seg_v[0:CAP, d : d + 1] for d in slots], axis=0)
        scores = lax.dot_general(
            block, keys, (((1,), (1,)), ((), ())), preferred_element_type=jnp.float32
        )
        scores = jnp.where(seg == seg_k, scores, -1e30)
        top = jnp.max(scores, axis=1, keepdims=True)
        powers = jnp.exp2((scores - top) * SCALE).astype(jnp.bfloat16)
        both = jnp.dot(powers, values, preferred_element_type=jnp.float32)
        attended = both[:, :HEAD_DIM] / both[:, HEAD_DIM:]
        attended = jnp.where(seg >= 0.0, attended, 0.0)
        c_v[first : first + BATCH] = attended.astype(jnp.bfloat16).reshape(BATCH, CAP, HEAD_DIM)
        squares = squares + jnp.sum(
            (attended * attended).reshape(BATCH * CAP // 8, 8, HEAD_DIM), axis=0
        )
        for d in slots:
            if d == 0:
                own_c.start()
            else:
                context_copy(d).start()

    def add_up(value, slots_ref, send_sem, recv_sem, count, peer):
        slots_ref[0] = value

        def copy(d):
            return pltpu.make_async_remote_copy(
                src_ref=slots_ref.at[0],
                dst_ref=slots_ref.at[d],
                send_sem=send_sem.at[d],
                recv_sem=recv_sem.at[d],
                device_id=peer(d),
                device_id_type=MESH,
            )

        for d in range(1, count):
            copy(d).start()
        for d in range(1, count):
            copy(d).wait_recv()
        out = jnp.sum(slots_ref[...], axis=0)
        return out, [copy(d) for d in range(1, count)]

    squares, sent1 = add_up(squares, r1, s1_sem, t1_sem, ni, in_peer)
    squares, sent2 = add_up(squares, r2, s2_sem, t2_sem, no, out_peer)
    squares, sent3 = add_up(squares, r3, s3_sem, t3_sem, ng, grp_peer)
    width = jnp.float32(HEAD_DIM * nm)
    var[...] = jnp.full(
        var.shape, jnp.sum(squares) / (width * live_rows.astype(jnp.float32)), jnp.float32
    )

    own_c.wait()
    for d in range(1, ng):
        query_copy(d).wait_send()
        context_copy(d).wait()
    for copy in sent1 + sent2 + sent3:
        copy.wait_send()


def per_device(ng, nm, enc_out, w_key, w_value, queries, src_len, tgt_len, destination):
    ni = math.gcd(nm, 8) if nm > 8 else max(nm // 2, 1)
    no = nm // ni
    rows, depth = enc_out.shape
    hbm = pl.BlockSpec(memory_space=pltpu.HBM)
    dma = pltpu.SemaphoreType.DMA
    context, variance = pl.pallas_call(
        functools.partial(kernel, ng, nm, ni),
        name="attend",
        out_shape=(
            jax.ShapeDtypeStruct(queries.shape, jnp.bfloat16),
            jax.ShapeDtypeStruct((1, 1), jnp.float32),
        ),
        in_specs=[hbm] * 7,
        out_specs=(pl.BlockSpec(memory_space=pl.ANY), pl.BlockSpec(memory_space=pltpu.VMEM)),
        scratch_shapes=[
            pltpu.VMEM((CHUNKS, rows, depth // CHUNKS), jnp.bfloat16),
            pltpu.VMEM((depth, 2 * HEAD_DIM), jnp.bfloat16),
            pltpu.VMEM((ng, CAP, HEAD_DIM), jnp.bfloat16),
            pltpu.VMEM((ng, CAP, HEAD_DIM), jnp.bfloat16),
            pltpu.VMEM((128, 16), jnp.float32),
            pltpu.VMEM((ni, 8, HEAD_DIM), jnp.float32),
            pltpu.VMEM((no, 8, HEAD_DIM), jnp.float32),
            pltpu.VMEM((ng, 8, HEAD_DIM), jnp.float32),
            pltpu.SMEM(src_len.shape, jnp.int32),
            pltpu.SMEM(tgt_len.shape, jnp.int32),
            pltpu.SMEM((1, destination.shape[0]), jnp.int32),
            dma((3, CHUNKS)), dma((3,)), dma((ng,)), dma((ng,)), dma((ng,)), dma((ng,)), dma((2,)),
            dma((ni,)), dma((ni,)), dma((no,)), dma((no,)), dma((ng,)), dma((ng,)),
        ],
        compiler_params=pltpu.CompilerParams(
            collective_id=0, has_side_effects=True, vmem_limit_bytes=56 << 20
        ),
        cost_estimate=pl.CostEstimate(
            flops=4 * rows * depth * HEAD_DIM, bytes_accessed=12 << 20, transcendentals=1 << 19
        ),
    )(enc_out, w_key, w_value, queries, src_len, tgt_len, destination.reshape(1, -1))
    return context, variance.reshape(())


def solution(mesh):
    return jax.shard_map(
        functools.partial(per_device, mesh.shape["grp"], mesh.shape["mdl"]),
        mesh=mesh,
        in_specs=(P("grp", None), P(None, "mdl"), P(None, "mdl"), P("grp", "mdl"), P(), P(), P()),
        out_specs=(P("grp", "mdl"), P()),
        check_vma=False,
    )
```

time: 213 us -> 63 us (0.30)
  the two profiles are of different devices: /device:TPU:1 before, /device:TPU:8 now
where the time goes in v1:
time: 63 us; the launch traced here: 62.8 us
  Pallas kernels  58.6 us (93%)
  between operations  2.39 us (4%)
  local copies, waits for them, and re-layouts  1.77 us (3%)
    pallas_call x1, Pallas kernels, per_device(): pl.pallas_call(functools.partial(kernel, ng, nm, ni), name='attend', out_...  58.6 us
    unnamed x1, local copies, waits for them, and re-layouts  1.77 us

profile of v1, /device:TPU:8, one launch (start us, length us, event | category | flops | bytes accessed | tf_op | source)
XLA Modules:
  0.0 62.8 jit_solution(11208464084421000887)
XLA Ops:
  0.6 58.6 %attend.1 = (bf16[1536,128]{1,0:T(8,128)(2,1)}, f32[1,1]{1,0:T(1,128)}) custom-call(bf16[320,8192]{1,0:T(8,128)(2,1)} %enc.1, bf16[8192,128]{1,0:T(8,128)(2,1)} %wk.1, bf16[8192,128]{1,0:T(8,128)(2,1)} %wv.1, bf16[1536,128]{1,0:T(8,128)(2,1)} %q.1, s32[16,19]{1,0:T(8,128)} %src.1, s32[304]{0:T(512)} %tgt.1, s32[1,304]{1,0:T(1,128)} %bitcast.2), custom_call_target="tpu_custom_call" | custom-call | flops 1342177280 | bytes 12582912 | tf_op jit(solution)/shard_map/attend/pallas_call | solution.py:217
  59.3 1.8 %copy.11 = bf16[1536,128]{1,0:T(8,128)(2,1)} copy(bf16[1536,128]{1,0:T(8,128)(2,1)} %get-tuple-element.8) | data formatting | bytes 786432

commit v2 on v1

--- a/solution.py
+++ b/solution.py
@@ -18,18 +18,45 @@
 
 
 def kernel(
-    ng, nm, ni,
+    ng, nz,
     enc, wk, wv, q, src, tgt, dst,
     ctx, var,
-    enc_v, w_v, q_v, c_v, seg_v, r1, r2, r3, src_s, tgt_s, dst_s,
+    enc_v, w_v, q_v, c_v, seg_v, plane_v, line_v, src_s, tgt_s, dst_s,
     load_sem, small_sem, qs_sem, qr_sem, cs_sem, cr_sem, own_sem,
-    s1_sem, t1_sem, s2_sem, t2_sem, s3_sem, t3_sem,
+    ps_sem, pr_sem, ls_sem, lr_sem, near_sem,
 ):
     me = lax.axis_index("grp")
     mm = lax.axis_index("mdl")
     rows, depth = enc.shape
     kc = depth // CHUNKS
-    no = nm // ni
+    z, core = mm // 2, lax.rem(mm, 2)
+
+    def plane_peer(i):
+        return {"grp": lax.rem(me + i % ng, ng), "mdl": z * 2 + lax.rem(core + i // ng, 2)}
+
+    def line_peer(d):
+        return {"mdl": lax.rem(z + d, nz) * 2 + core}
+
+    def tell(sem, peer):
+        pl.semaphore_signal(sem, inc=1, device_id=peer, device_id_type=MESH)
+
+    barrier = pltpu.get_barrier_semaphore()
+    for i in range(1, 2 * ng):
+        tell(barrier, plane_peer(i))
+    ends = sorted({1, nz - 1})
+    for d in ends:
+        tell(barrier, line_peer(d))
+
+    steps = [2**k for k in range(max(nz.bit_length() - 2, 0))]
+
+    def spread(k):
+        for d in sorted({steps[k], nz - steps[k]}):
+            tell(near_sem.at[k], line_peer(d))
+
+    def heard(k):
+        pl.semaphore_wait(near_sem.at[k], len({steps[k], nz - steps[k]}))
+        if k + 1 < len(steps):
+            spread(k + 1)
 
     small = [
         pltpu.make_async_copy(a, b, small_sem.at[i])
@@ -55,25 +82,7 @@
         for copy in loads(c):
             copy.start()
 
-    def grp_peer(d):
-        return {"grp": lax.rem(me + d, ng)}
-
-    inner, outer = lax.rem(mm, ni), mm // ni
-
-    def in_peer(d):
-        return {"mdl": outer * ni + lax.rem(inner + d, ni)}
-
-    def out_peer(d):
-        return {"mdl": lax.rem(outer + d, no) * ni + inner}
-
-    barrier = pltpu.get_barrier_semaphore()
-    for d in range(1, ng):
-        pl.semaphore_signal(barrier, inc=1, device_id=grp_peer(d), device_id_type=MESH)
-    for d in range(1, ni):
-        pl.semaphore_signal(barrier, inc=1, device_id=in_peer(d), device_id_type=MESH)
-    for d in range(1, no):
-        pl.semaphore_signal(barrier, inc=1, device_id=out_peer(d), device_id_type=MESH)
-    pl.semaphore_wait(barrier, (ng - 1) + (ni - 1) + (no - 1))
+    pl.semaphore_wait(barrier, 2 * ng - 1 + len(ends))
 
     def query_copy(d):
         peer = lax.rem(me + d, ng)
@@ -88,6 +97,8 @@
 
     for d in range(1, ng):
         query_copy(d).start()
+    if steps:
+        spread(0)
 
     for copy in small:
         copy.wait()
@@ -120,6 +131,10 @@
         0, tgt.shape[0], lambda i, t: t + tgt_s[i], jnp.int32(0), unroll=8
     )
 
+    pending = list(range(len(steps)))
+    if pending:
+        heard(pending.pop(0))
+
     total = jnp.zeros((rows, 2 * HEAD_DIM), jnp.float32)
     for c in range(CHUNKS):
         for copy in loads(c):
@@ -127,6 +142,8 @@
         total = total + jnp.dot(
             enc_v[c], w_v[pl.ds(c * kc, kc), :], preferred_element_type=jnp.float32
         )
+        if c % 4 == 3 and len(pending) > 1:
+            heard(pending.pop(0))
     keys = total[:, :HEAD_DIM].astype(jnp.bfloat16)
     values = jnp.concatenate(
         [total[:, HEAD_DIM:].astype(jnp.bfloat16), jnp.ones((rows, HEAD_DIM), jnp.bfloat16)], axis=1
@@ -166,56 +183,59 @@
         squares = squares + jnp.sum(
             (attended * attended).reshape(BATCH * CAP // 8, 8, HEAD_DIM), axis=0
         )
-        for d in slots:
-            if d == 0:
-                own_c.start()
-            else:
-                context_copy(d).start()
-
-    def add_up(value, slots_ref, send_sem, recv_sem, count, peer):
-        slots_ref[0] = value
-
-        def copy(d):
-            return pltpu.make_async_remote_copy(
-                src_ref=slots_ref.at[0],
-                dst_ref=slots_ref.at[d],
-                send_sem=send_sem.at[d],
-                recv_sem=recv_sem.at[d],
-                device_id=peer(d),
-                device_id_type=MESH,
-            )
-
-        for d in range(1, count):
-            copy(d).start()
-        for d in range(1, count):
-            copy(d).wait_recv()
-        out = jnp.sum(slots_ref[...], axis=0)
-        return out, [copy(d) for d in range(1, count)]
-
-    squares, sent1 = add_up(squares, r1, s1_sem, t1_sem, ni, in_peer)
-    squares, sent2 = add_up(squares, r2, s2_sem, t2_sem, no, out_peer)
-    squares, sent3 = add_up(squares, r3, s3_sem, t3_sem, ng, grp_peer)
-    width = jnp.float32(HEAD_DIM * nm)
-    var[...] = jnp.full(
-        var.shape, jnp.sum(squares) / (width * live_rows.astype(jnp.float32)), jnp.float32
-    )
-
+
+    def add_copy(held, row, send_sem, recv_sem, d, peer):
+        return pltpu.make_async_remote_copy(
+            src_ref=held.at[row],
+            dst_ref=held.at[row],
+            send_sem=send_sem.at[d],
+            recv_sem=recv_sem.at[d],
+            device_id=peer,
+            device_id_type=MESH,
+        )
+
+    def plane_copy(i):
+        return add_copy(plane_v, core * ng + me, ps_sem, pr_sem, i, plane_peer(i))
+
+    def line_copy(d):
+        return add_copy(line_v, z, ls_sem, lr_sem, d, line_peer(d))
+
+    plane_v[core * ng + me] = jnp.sum(squares, axis=0, keepdims=True)
+    for i in range(1, 2 * ng):
+        plane_copy(i).start()
+    own_c.start()
+    for d in range(1, ng):
+        context_copy(d).start()
+    while pending:
+        heard(pending.pop(0))
+    for i in range(1, 2 * ng):
+        plane_copy(i).wait_recv()
+    line_v[z] = jnp.sum(plane_v[...], axis=0)
+    order = sorted(range(1, nz), key=lambda d: -min(d, nz - d))
+    for d in order:
+        line_copy(d).start()
+
+    for i in range(1, 2 * ng):
+        plane_copy(i).wait_send()
     own_c.wait()
     for d in range(1, ng):
         query_copy(d).wait_send()
         context_copy(d).wait()
-    for copy in sent1 + sent2 + sent3:
-        copy.wait_send()
+    for d in range(1, nz):
+        line_copy(d).wait()
+    width = jnp.float32(HEAD_DIM * 2 * nz)
+    var[...] = jnp.full(
+        var.shape, jnp.sum(line_v[...]) / (width * live_rows.astype(jnp.float32)), jnp.float32
+    )
 
 
 def per_device(ng, nm, enc_out, w_key, w_value, queries, src_len, tgt_len, destination):
-    ni = math.gcd(nm, 8) if nm > 8 else max(nm // 2, 1)
-    no = nm // ni
+    nz = nm // 2
     rows, depth = enc_out.shape
     hbm = pl.BlockSpec(memory_space=pltpu.HBM)
     dma = pltpu.SemaphoreType.DMA
     context, variance = pl.pallas_call(
-        functools.partial(kernel, ng, nm, ni),
+        functools.partial(kernel, ng, nz),
         name="attend",
         out_shape=(
             jax.ShapeDtypeStruct(queries.shape, jnp.bfloat16),
@@ -229,14 +249,14 @@
             pltpu.VMEM((ng, CAP, HEAD_DIM), jnp.bfloat16),
             pltpu.VMEM((ng, CAP, HEAD_DIM), jnp.bfloat16),
             pltpu.VMEM((128, 16), jnp.float32),
-            pltpu.VMEM((ni, 8, HEAD_DIM), jnp.float32),
-            pltpu.VMEM((no, 8, HEAD_DIM), jnp.float32),
-            pltpu.VMEM((ng, 8, HEAD_DIM), jnp.float32),
+            pltpu.VMEM((2 * ng, 1, HEAD_DIM), jnp.float32),
+            pltpu.VMEM((nz, 1, HEAD_DIM), jnp.float32),
             pltpu.SMEM(src_len.shape, jnp.int32),
             pltpu.SMEM(tgt_len.shape, jnp.int32),
             pltpu.SMEM((1, destination.shape[0]), jnp.int32),
             dma((3, CHUNKS)), dma((3,)), dma((ng,)), dma((ng,)), dma((ng,)), dma((ng,)), dma((2,)),
-            dma((ni,)), dma((ni,)), dma((no,)), dma((no,)), dma((ng,)), dma((ng,)),
+            dma((2 * ng,)), dma((2 * ng,)), dma((nz,)), dma((nz,)),
+            pltpu.SemaphoreType.REGULAR((max(nz.bit_length() - 2, 1),)),
         ],
         compiler_params=pltpu.CompilerParams(
             collective_id=0, has_side_effects=True, vmem_limit_bytes=56 << 20

time: 63 us -> 56.4 us (0.90)
  the two profiles are of different devices: /device:TPU:8 before, /device:TPU:1 now
where the time goes in v2:
time: 56.4 us; the launch traced here: 56.2 us
  Pallas kernels  52.1 us (92%)
  between operations  2.39 us (4%)
  local copies, waits for them, and re-layouts  1.77 us (3%)
    pallas_call x1, Pallas kernels, per_device(): pl.pallas_call(functools.partial(kernel, ng, nz), name='attend', out_shap...  52.1 us
    unnamed x1, local copies, waits for them, and re-layouts  1.77 us

profile of v2, /device:TPU:1, one launch (start us, length us, event | category | flops | bytes accessed | tf_op | source)
XLA Modules:
  0.0 56.2 jit_solution(6931889558878867004)
XLA Ops:
  0.6 52.1 %attend.1 = (bf16[1536,128]{1,0:T(8,128)(2,1)}, f32[1,1]{1,0:T(1,128)}) custom-call(bf16[320,8192]{1,0:T(8,128)(2,1)} %enc.1, bf16[8192,128]{1,0:T(8,128)(2,1)} %wk.1, bf16[8192,128]{1,0:T(8,128)(2,1)} %wv.1, bf16[1536,128]{1,0:T(8,128)(2,1)} %q.1, s32[16,19]{1,0:T(8,128)} %src.1, s32[304]{0:T(512)} %tgt.1, s32[1,304]{1,0:T(1,128)} %bitcast.2), custom_call_target="tpu_custom_call" | custom-call | flops 1342177280 | bytes 12582912 | tf_op jit(solution)/shard_map/attend/pallas_call | solution.py:237
  52.7 1.8 %copy.11 = bf16[1536,128]{1,0:T(8,128)(2,1)} copy(bf16[1536,128]{1,0:T(8,128)(2,1)} %get-tuple-element.8) | data formatting | bytes 786432

commit v3 on v2

v3 whole, which is shorter than its diff:
```python
import functools
import math

import jax
import jax.numpy as jnp
from jax import lax
from jax.experimental import pallas as pl
from jax.experimental.pallas import tpu as pltpu
from jax.sharding import PartitionSpec as P

HEAD_DIM = 128
CAP = 96
SENTS = 19
CHUNKS = 8
EARLY = 2
NEAR = 4
MESH = pl.DeviceIdType.MESH
SCALE = math.log2(math.e) * HEAD_DIM**-0.5


def kernel(
    ng, nz,
    enc, wk, wv, q, src, tgt, dst,
    ctx, var,
    enc_v, w_v, q_v, c_v, pick_v, plane_v, line_v, src_s, tgt_s, dst_s,
    load_sem, small_sem, qs_sem, qr_sem, cs_sem, cr_sem, own_sem,
    ps_sem, pr_sem, ls_sem, lr_sem, near_sem,
):
    me = lax.axis_index("grp")
    mm = lax.axis_index("mdl")
    rows, depth = enc.shape
    kc = depth // CHUNKS
    z, core = mm // 2, lax.rem(mm, 2)

    side = math.isqrt(ng)
    y, x = me // side, lax.rem(me, side)

    def ahead(d):
        return lax.rem(y + d // side, side) * side + lax.rem(x + d % side, side)

    def behind(d):
        dy, dx = lax.div(d, side), lax.rem(d, side)
        return lax.rem(y + side - dy, side) * side + lax.rem(x + side - dx, side)

    def hops(d):
        dy, dx = d % ng // side, d % side
        return min(dy, side - dy) + min(dx, side - dx)

    far_groups = sorted(range(1, ng), key=hops, reverse=True)
    far_plane = sorted(range(1, 2 * ng), key=hops, reverse=True)

    def plane_peer(i):
        return {"grp": ahead(i % ng), "mdl": z * 2 + lax.rem(core + i // ng, 2)}

    def line_peer(d):
        return {"mdl": lax.rem(z + d, nz) * 2 + core}

    def tell(sem, peer):
        pl.semaphore_signal(sem, inc=1, device_id=peer, device_id_type=MESH)

    near = min(NEAR, nz // 2)

    def at_distance(k):
        return sorted({k, nz - k})

    close = [d for k in range(near, 0, -1) for d in at_distance(k)]
    barrier = pltpu.get_barrier_semaphore()
    for i in far_plane[: len(far_plane) // 2]:
        tell(barrier, plane_peer(i))
    for d in close:
        tell(barrier, line_peer(d))
    for i in far_plane[len(far_plane) // 2 :]:
        tell(barrier, plane_peer(i))

    steps = [near << k for k in range(nz.bit_length()) if (near << k) < nz // 2]

    def spread(k):
        for d in at_distance(steps[k]):
            tell(near_sem.at[k], line_peer(d))

    def heard(k):
        if k < len(steps):
            pl.semaphore_wait(near_sem.at[k], len(at_distance(steps[k])))
            if k + 1 < len(steps):
                spread(k + 1)

    small = [
        pltpu.make_async_copy(a, b, small_sem.at[i])
        for i, (a, b) in enumerate(((src, src_s), (tgt, tgt_s), (dst, dst_s)))
    ]
    for copy in small:
        copy.start()

    def loads(c):
        part = pl.ds(c * kc, kc)
        return (
            pltpu.make_async_copy(enc.at[:, part], enc_v.at[c], load_sem.at[0, c]),
            pltpu.make_async_copy(wk.at[part], w_v.at[part, pl.ds(0, HEAD_DIM)], load_sem.at[1, c]),
            pltpu.make_async_copy(
                wv.at[part], w_v.at[part, pl.ds(HEAD_DIM, HEAD_DIM)], load_sem.at[2, c]
            ),
        )

    own_rows = pl.ds(pl.multiple_of(me * CAP, 32), CAP)
    own_q = pltpu.make_async_copy(q.at[own_rows], q_v.at[0], own_sem.at[0])
    own_q.start()
    for c in range(CHUNKS):
        for copy in loads(c):
            copy.start()

    def query_copy(d):
        peer = ahead(d)
        return pltpu.make_async_remote_copy(
            src_ref=q.at[pl.ds(pl.multiple_of(peer * CAP, 32), CAP)],
            dst_ref=q_v.at[d],
            send_sem=qs_sem.at[d],
            recv_sem=qr_sem.at[d],
            device_id={"grp": peer},
            device_id_type=MESH,
        )

    for copy in small:
        copy.wait()
    slot = lax.broadcasted_iota(jnp.int32, (ng, 128), 0)
    lane = lax.broadcasted_iota(jnp.int32, (ng, 128), 1)
    group_of = behind(slot)
    key_row = lax.broadcasted_iota(jnp.int32, (1, rows), 1)
    target_row = lax.broadcasted_iota(jnp.int32, (rows, 1), 0)
    place = jnp.full(slot.shape, -1, jnp.int32)
    seg_k = jnp.zeros((1, rows), jnp.int32)
    seg_q = jnp.zeros((rows, 1), jnp.int32)
    filled = jnp.zeros(slot.shape, jnp.int32)
    start = jnp.int32(0)
    first = jnp.int32(0)
    for i in range(SENTS):
        count = tgt_s[me * SENTS + i]
        going = group_of == dst_s[0, me * SENTS + i]
        after = jnp.where(going, filled + count, filled)
        place = jnp.where((lane >= filled) & (lane < after), lane - filled + first, place)
        filled = after
        seg_k = jnp.where(key_row >= start, i, seg_k)
        seg_q = jnp.where(target_row >= first, i, seg_q)
        start = start + src_s[me, i]
        first = first + count
    place = place.astype(jnp.float32)
    across = place.T
    order_row = lax.broadcasted_iota(jnp.int32, (rows, CAP), 0).astype(jnp.float32)
    for d in range(ng):
        pick_v[d] = jnp.where(order_row == place[d : d + 1, :CAP], 1.0, 0.0).astype(jnp.bfloat16)
    live_rows = lax.fori_loop(
        0, tgt.shape[0], lambda i, t: t + tgt_s[i], jnp.int32(0), unroll=8
    )

    total = jnp.zeros((rows, 2 * HEAD_DIM), jnp.float32)
    for c in range(CHUNKS):
        if c == EARLY:
            pl.semaphore_wait(barrier, 2 * ng - 1 + len(close))
            for d in far_groups:
                query_copy(d).start()
            if steps:
                spread(0)
        for copy in loads(c):
            copy.wait()
        total = total + jnp.dot(
            enc_v[c], w_v[pl.ds(c * kc, kc), :], preferred_element_type=jnp.float32
        )
    heard(0)
    keys = total[:, :HEAD_DIM].astype(jnp.bfloat16)
    values = jnp.concatenate(
        [total[:, HEAD_DIM:].astype(jnp.bfloat16), jnp.ones((rows, HEAD_DIM), jnp.bfloat16)], axis=1
    )

    def context_copy(d):
        return pltpu.make_async_remote_copy(
            src_ref=c_v.at[d],
            dst_ref=ctx.at[own_rows],
            send_sem=cs_sem.at[d],
            recv_sem=cr_sem.at[d],
            device_id={"grp": behind(d)},
            device_id_type=MESH,
        )

    gathered = jnp.zeros((rows, HEAD_DIM), jnp.float32)
    for d in [0] + far_groups[::-1]:
        if d == 0:
            own_q.wait()
        else:
            query_copy(d).wait_recv()
        gathered = gathered + jnp.dot(pick_v[d], q_v[d], preferred_element_type=jnp.float32)
    scores = lax.dot_general(
        gathered.astype(jnp.bfloat16), keys, (((1,), (1,)), ((), ())),
        preferred_element_type=jnp.float32,
    )
    scores = jnp.where(seg_q == seg_k, scores, -1e30)
    top = jnp.max(scores, axis=1, keepdims=True)
    powers = jnp.exp2((scores - top) * SCALE).astype(jnp.bfloat16)
    both = jnp.dot(powers, values, preferred_element_type=jnp.float32)
    attended = both[:, :HEAD_DIM] / both[:, HEAD_DIM:]
    attended = jnp.where(target_row < first, attended, 0.0)
    squares = attended * attended

    def add_copy(held, row, send_sem, recv_sem, d, peer):
        return pltpu.make_async_remote_copy(
            src_ref=held.at[row],
            dst_ref=held.at[row],
            send_sem=send_sem.at[d],
            recv_sem=recv_sem.at[d],
            device_id=peer,
            device_id_type=MESH,
        )

    def plane_copy(i):
        return add_copy(plane_v, core * ng + me, ps_sem, pr_sem, i, plane_peer(i))

    def line_copy(d):
        return add_copy(line_v, z, ls_sem, lr_sem, d, line_peer(d))

    plane_v[core * ng + me] = jnp.sum(squares, axis=0, keepdims=True)
    for i in far_plane:
        plane_copy(i).start()
    own_c = pltpu.make_async_copy(c_v.at[0], ctx.at[own_rows], own_sem.at[1])
    attended = attended.astype(jnp.bfloat16)
    order_lane = lax.broadcasted_iota(jnp.int32, (CAP, rows), 1).astype(jnp.float32)
    for d in far_groups + [0]:
        spread_out = jnp.where(order_lane == across[:CAP, d : d + 1], 1.0, 0.0)
        c_v[d] = jnp.dot(
            spread_out.astype(jnp.bfloat16), attended, preferred_element_type=jnp.float32
        ).astype(jnp.bfloat16)
        if d == 0:
            own_c.start()
        else:
            context_copy(d).start()
    for i in range(1, 2 * ng):
        plane_copy(i).wait_recv()
    for k in range(1, len(steps)):
        heard(k)
    line_v[z] = jnp.sum(plane_v[...], axis=0)
    order = sorted(range(1, nz), key=lambda d: -min(d, nz - d))
    for d in order:
        line_copy(d).start()

    for i in range(1, 2 * ng):
        plane_copy(i).wait_send()
    own_c.wait()
    for d in range(1, ng):
        query_copy(d).wait_send()
        context_copy(d).wait()
    for d in range(1, nz):
        line_copy(d).wait()
    width = jnp.float32(HEAD_DIM * 2 * nz)
    var[...] = jnp.full(
        var.shape, jnp.sum(line_v[...]) / (width * live_rows.astype(jnp.float32)), jnp.float32
    )


def per_device(ng, nm, enc_out, w_key, w_value, queries, src_len, tgt_len, destination):
    nz = nm // 2
    rows, depth = enc_out.shape
    hbm = pl.BlockSpec(memory_space=pltpu.HBM)
    dma = pltpu.SemaphoreType.DMA
    context, variance = pl.pallas_call(
        functools.partial(kernel, ng, nz),
        name="attend",
        out_shape=(
            pltpu.VMEM(queries.shape, jnp.bfloat16),
            pltpu.VMEM((1, 1), jnp.float32),
        ),
        in_specs=[hbm] * 7,
        out_specs=(pl.BlockSpec(memory_space=pl.ANY), pl.BlockSpec(memory_space=pltpu.VMEM)),
        scratch_shapes=[
            pltpu.VMEM((CHUNKS, rows, depth // CHUNKS), jnp.bfloat16),
            pltpu.VMEM((depth, 2 * HEAD_DIM), jnp.bfloat16),
            pltpu.VMEM((ng, CAP, HEAD_DIM), jnp.bfloat16),
            pltpu.VMEM((ng, CAP, HEAD_DIM), jnp.bfloat16),
            pltpu.VMEM((ng, rows, CAP), jnp.bfloat16),
            pltpu.VMEM((2 * ng, 1, HEAD_DIM), jnp.float32),
            pltpu.VMEM((nz, 1, HEAD_DIM), jnp.float32),
            pltpu.SMEM(src_len.shape, jnp.int32),
            pltpu.SMEM(tgt_len.shape, jnp.int32),
            pltpu.SMEM((1, destination.shape[0]), jnp.int32),
            dma((3, CHUNKS)), dma((3,)), dma((ng,)), dma((ng,)), dma((ng,)), dma((ng,)), dma((2,)),
            dma((2 * ng,)), dma((2 * ng,)), dma((nz,)), dma((nz,)),
            pltpu.SemaphoreType.REGULAR((nz.bit_length(),)),
        ],
        compiler_params=pltpu.CompilerParams(
            collective_id=0, has_side_effects=True, vmem_limit_bytes=56 << 20
        ),
        cost_estimate=pl.CostEstimate(
            flops=4 * rows * depth * HEAD_DIM, bytes_accessed=12 << 20, transcendentals=1 << 19
        ),
    )(enc_out, w_key, w_value, queries, src_len, tgt_len, destination.reshape(1, -1))
    return context, variance.reshape(())


def solution(mesh):
    return jax.shard_map(
        functools.partial(per_device, mesh.shape["grp"], mesh.shape["mdl"]),
        mesh=mesh,
        in_specs=(P("grp", None), P(None, "mdl"), P(None, "mdl"), P("grp", "mdl"), P(), P(), P()),
        out_specs=(P("grp", "mdl"), P()),
        check_vma=False,
    )
```

time: 56.4 us -> 53.5 us (0.949)
  Pallas kernels: 52.1 us -> 50.8 us
  local copies, waits for them, and re-layouts: 1.77 us -> 0.75 us
  between operations: 2.39 us -> 1.8 us
    pallas_call x1, Pallas kernels: 52.1 us -> 50.8 us  [per_device(): pl.pallas_call(functools.partial(kernel, ng, nz), name='attend', out_shap...]
    unnamed x1, local copies, waits for them, and re-layouts: 1.77 us -> 0.75 us
where the time goes in v3:
time: 53.5 us; the launch traced here: 53.3 us
  Pallas kernels  50.8 us (95%)
  between operations  1.8 us (3%)
  local copies, waits for them, and re-layouts  0.75 us (1%)
    pallas_call x1, Pallas kernels, per_device(): pl.pallas_call(functools.partial(kernel, ng, nz), name='attend', out_shap...  50.8 us

profile of v3, /device:TPU:1, one launch (start us, length us, event | category | flops | bytes accessed | tf_op | source)
XLA Modules:
  0.0 53.3 jit_solution(8067692863252766937)
XLA Ops:
  0.6 50.8 %attend.1 = (bf16[1536,128]{1,0:T(8,128)(2,1)S(1)}, f32[1,1]{1,0:T(1,128)S(1)}) custom-call(bf16[320,8192]{1,0:T(8,128)(2,1)} %enc.1, bf16[8192,128]{1,0:T(8,128)(2,1)} %wk.1, bf16[8192,128]{1,0:T(8,128)(2,1)} %wv.1, bf16[1536,128]{1,0:T(8,128)(2,1)} %q.1, s32[16,19]{1,0:T(8,128)} %src.1, s32[304]{0:T(512)} %tgt.1, s32[1,304]{1,0:T(1,128)} %bitcast.2), custom_call_target="tpu_custom_call" | custom-call | flops 1342177280 | bytes 12582912 | tf_op jit(solution)/shard_map/attend/pallas_call | solution.py:261
  51.4 0.7 %copy.11 = bf16[1536,128]{1,0:T(8,128)(2,1)} copy(bf16[1536,128]{1,0:T(8,128)(2,1)S(1)} %get-tuple-element.6) | data formatting | bytes 786432

commit v4 on v3

--- a/solution.py
+++ b/solution.py
@@ -12,7 +12,6 @@
 CAP = 96
 SENTS = 19
 CHUNKS = 8
-EARLY = 2
 NEAR = 4
 MESH = pl.DeviceIdType.MESH
 SCALE = math.log2(math.e) * HEAD_DIM**-0.5
@@ -24,7 +23,7 @@
     ctx, var,
     enc_v, w_v, q_v, c_v, pick_v, plane_v, line_v, src_s, tgt_s, dst_s,
     load_sem, small_sem, qs_sem, qr_sem, cs_sem, cr_sem, own_sem,
-    ps_sem, pr_sem, ls_sem, lr_sem, near_sem,
+    ps_sem, pr_sem, ls_sem, lr_sem, near_sem, core_sem,
 ):
     me = lax.axis_index("grp")
     mm = lax.axis_index("mdl")
@@ -34,9 +33,11 @@
 
     side = math.isqrt(ng)
     y, x = me // side, lax.rem(me, side)
+    ys = [lax.rem(y + k, side) * side for k in range(side)]
+    xs = [lax.rem(x + k, side) for k in range(side)]
 
     def ahead(d):
-        return lax.rem(y + d // side, side) * side + lax.rem(x + d % side, side)
+        return ys[d // side] + xs[d % side]
 
     def behind(d):
         dy, dx = lax.div(d, side), lax.rem(d, side)
@@ -50,7 +51,7 @@
     far_plane = sorted(range(1, 2 * ng), key=hops, reverse=True)
 
     def plane_peer(i):
-        return {"grp": ahead(i % ng), "mdl": z * 2 + lax.rem(core + i // ng, 2)}
+        return {"grp": ahead(i % ng), "mdl": mm if i < ng else z * 2 + 1 - core}
 
     def line_peer(d):
         return {"mdl": lax.rem(z + d, nz) * 2 + core}
@@ -65,12 +66,10 @@
 
     close = [d for k in range(near, 0, -1) for d in at_distance(k)]
     barrier = pltpu.get_barrier_semaphore()
-    for i in far_plane[: len(far_plane) // 2]:
+    for i in far_groups + [ng]:
         tell(barrier, plane_peer(i))
     for d in close:
         tell(barrier, line_peer(d))
-    for i in far_plane[len(far_plane) // 2 :]:
-        tell(barrier, plane_peer(i))
 
     steps = [near << k for k in range(nz.bit_length()) if (near << k) < nz // 2]
 
@@ -128,7 +127,7 @@
     target_row = lax.broadcasted_iota(jnp.int32, (rows, 1), 0)
     place = jnp.full(slot.shape, -1, jnp.int32)
     seg_k = jnp.zeros((1, rows), jnp.int32)
-    seg_q = jnp.zeros((rows, 1), jnp.int32)
+    begins = []
     filled = jnp.zeros(slot.shape, jnp.int32)
     start = jnp.int32(0)
     first = jnp.int32(0)
@@ -139,31 +138,34 @@
         place = jnp.where((lane >= filled) & (lane < after), lane - filled + first, place)
         filled = after
         seg_k = jnp.where(key_row >= start, i, seg_k)
-        seg_q = jnp.where(target_row >= first, i, seg_q)
+        begins.append((first, i))
         start = start + src_s[me, i]
         first = first + count
+
+    pl.semaphore_wait(barrier, ng + len(close))
+    for d in far_groups[::-1]:
+        query_copy(d).start()
+    tell(core_sem, plane_peer(ng))
+    if steps:
+        spread(0)
+
+    seg_q = jnp.zeros((rows, 1), jnp.int32)
+    for begin, i in begins:
+        seg_q = jnp.where(target_row >= begin, i, seg_q)
     place = place.astype(jnp.float32)
     across = place.T
     order_row = lax.broadcasted_iota(jnp.int32, (rows, CAP), 0).astype(jnp.float32)
     for d in range(ng):
         pick_v[d] = jnp.where(order_row == place[d : d + 1, :CAP], 1.0, 0.0).astype(jnp.bfloat16)
-    live_rows = lax.fori_loop(
-        0, tgt.shape[0], lambda i, t: t + tgt_s[i], jnp.int32(0), unroll=8
-    )
 
     total = jnp.zeros((rows, 2 * HEAD_DIM), jnp.float32)
     for c in range(CHUNKS):
-        if c == EARLY:
-            pl.semaphore_wait(barrier, 2 * ng - 1 + len(close))
-            for d in far_groups:
-                query_copy(d).start()
-            if steps:
-                spread(0)
         for copy in loads(c):
             copy.wait()
         total = total + jnp.dot(
             enc_v[c], w_v[pl.ds(c * kc, kc), :], preferred_element_type=jnp.float32
         )
+    pl.semaphore_wait(core_sem, 1)
     heard(0)
     keys = total[:, :HEAD_DIM].astype(jnp.bfloat16)
     values = jnp.concatenate(
@@ -238,6 +240,9 @@
     order = sorted(range(1, nz), key=lambda d: -min(d, nz - d))
     for d in order:
         line_copy(d).start()
+    live_rows = lax.fori_loop(
+        0, tgt.shape[0], lambda i, t: t + tgt_s[i], jnp.int32(0), unroll=8
+    )
 
     for i in range(1, 2 * ng):
         plane_copy(i).wait_send()
@@ -246,7 +251,9 @@
         query_copy(d).wait_send()
         context_copy(d).wait()
     for d in range(1, nz):
-        line_copy(d).wait()
+        line_copy(d).wait_send()
+    for d in order[::-1]:
+        line_copy(d).wait_recv()
     width = jnp.float32(HEAD_DIM * 2 * nz)
     var[...] = jnp.full(
         var.shape, jnp.sum(line_v[...]) / (width * live_rows.astype(jnp.float32)), jnp.float32
@@ -281,6 +288,7 @@
             dma((3, CHUNKS)), dma((3,)), dma((ng,)), dma((ng,)), dma((ng,)), dma((ng,)), dma((2,)),
             dma((2 * ng,)), dma((2 * ng,)), dma((nz,)), dma((nz,)),
             pltpu.SemaphoreType.REGULAR((nz.bit_length(),)),
+            pltpu.SemaphoreType.REGULAR,
         ],
         compiler_params=pltpu.CompilerParams(
             collective_id=0, has_side_effects=True, vmem_limit_bytes=56 << 20

time: 53.5 us -> 53 us (level)
  no operation moved by 1% of the time
where the time goes in v4:
time: 53 us; the launch traced here: 52.8 us
  Pallas kernels  50.3 us (95%)
  between operations  1.8 us (3%)
  local copies, waits for them, and re-layouts  0.75 us (1%)
    pallas_call x1, Pallas kernels, per_device(): pl.pallas_call(functools.partial(kernel, ng, nz), name='attend', out_shap...  50.3 us

profile of v4, /device:TPU:1, one launch (start us, length us, event | category | flops | bytes accessed | tf_op | source)
XLA Modules:
  0.0 52.8 jit_solution(4445913668337979036)
XLA Ops:
  0.6 50.3 %attend.1 = (bf16[1536,128]{1,0:T(8,128)(2,1)S(1)}, f32[1,1]{1,0:T(1,128)S(1)}) custom-call(bf16[320,8192]{1,0:T(8,128)(2,1)} %enc.1, bf16[8192,128]{1,0:T(8,128)(2,1)} %wk.1, bf16[8192,128]{1,0:T(8,128)(2,1)} %wv.1, bf16[1536,128]{1,0:T(8,128)(2,1)} %q.1, s32[16,19]{1,0:T(8,128)} %src.1, s32[304]{0:T(512)} %tgt.1, s32[1,304]{1,0:T(1,128)} %bitcast.2), custom_call_target="tpu_custom_call" | custom-call | flops 1342177280 | bytes 12582912 | tf_op jit(solution)/shard_map/attend/pallas_call | solution.py:268
  50.9 0.7 %copy.11 = bf16[1536,128]{1,0:T(8,128)(2,1)} copy(bf16[1536,128]{1,0:T(8,128)(2,1)S(1)} %get-tuple-element.6) | data formatting | bytes 786432
